TPU v7x, 32 devices: a whole 2x2x4 slice. The times are simulated.
32 devices in a mesh: seq: 4 (over y, x), fsdp: 8 (over z, core).
Axes of the slice: x: 2, y: 2, z: 4, core: 2. Of those that a mesh axis runs over, the one named last changes fastest.
Arguments:
- tokens: bfloat16 [8, 1024, 1536], P('fsdp', 'seq'), may hold values from -6 to 6
- mixing_weight: bfloat16 [1536, 2560], P(('seq', 'fsdp')), may hold values from -0.21875 to 0.21875
- output_weight: bfloat16 [1536, 1536], P(('seq', 'fsdp')), may hold values from -0.625 to 0.625
- norm_gains: bfloat16 [1536, 2], P(('seq', 'fsdp')), may hold values from 0.099609375 to 1.8984375
- expert_gate: bfloat16 [1536, 40, 512], P('fsdp', 'seq'), may hold values from -0.15625 to 0.15625
- expert_up: bfloat16 [1536, 40, 512], P('fsdp', 'seq'), may hold values from -0.15625 to 0.15625
- expert_down: bfloat16 [1536, 40, 512], P('fsdp', 'seq'), may hold values from -1.25 to 1.25
- gate_logits: float32 [8, 1024, 8], P('fsdp'), may hold values from -3 to 3
- routes: int32 [8, 1024, 8], P('fsdp'), may hold values from 0 to 39, all different within a row
- fill_order: int32 [8, 1024], P('fsdp'), may hold values from 0 to 1023, each once within a row
- cotangent: bfloat16 [8, 1024, 1536], P('fsdp', 'seq'), may hold values from -6 to 6
Outputs:
- layer_output: bfloat16 [8, 1024, 1536], P('fsdp', 'seq')
- tokens_gradient: float32 [8, 1024, 1536], P('fsdp', 'seq')
- mixing_gradient: float32 [1536, 2560], P(('seq', 'fsdp'))
- output_gradient: float32 [1536, 1536], P(('seq', 'fsdp'))
- gains_gradient: float32 [1536, 2], P(('seq', 'fsdp'))
- gate_gradient: float32 [1536, 40, 512], P('fsdp', 'seq')
- up_gradient: float32 [1536, 40, 512], P('fsdp', 'seq')
- down_gradient: float32 [1536, 40, 512], P('fsdp', 'seq')
- logits_gradient: float32 [8, 1024, 8], P('fsdp', 'seq')
Inputs may be any that keep to these rules, and one draw needn't show every extreme that they name: `routes`: each token names 8 different experts. `fill_order`: each sequence's row holds each token index of that sequence once.
All inputs are finite; a program needn't handle non-finite values.
Results may differ from a plain program's by a relative error of at most 0.017.
The roundings to bfloat16 on the way count: a program that leaves them out, or rounds other values in their place, can miss the bound.
Values may be sent and summed in bfloat16 or wider, within the bound.
A program may use at most 256 MiB of HBM per device.

v0:
```python
import math
import jax
import jax.numpy as jnp
from jax import lax
from jax.sharding import PartitionSpec as P

D = 1536
HEADS = 24
KV_HEADS = 8
HEAD_DIM = 64
FF = 512
EXPERTS = 40
TOP = 8
QBLK = 512
epsilon = 1e-05
rope_base = 10000.0


def norm_apply(values, gain_row):
    return (
        values * lax.rsqrt(jnp.mean(values * values, axis=-1, keepdims=True) + epsilon) * gain_row
    )


def rotary_tables(positions):
    half_width = HEAD_DIM // 2
    frequency = rope_base ** (-2.0 * jnp.arange(half_width, dtype=jnp.float32) / HEAD_DIM)
    angles = positions.astype(jnp.float32)[:, None] * frequency[None, :]
    cos_table = jnp.cos(angles)
    sin_table = jnp.sin(angles)
    return (jnp.concatenate([cos_table, cos_table], 1), jnp.concatenate([sin_table, sin_table], 1))


def rotate(values, cos_table, sin_table):
    half_width = values.shape[-1] // 2
    turned = jnp.concatenate([-values[..., half_width:], values[..., :half_width]], -1)
    return values * cos_table[:, None, :] + turned * sin_table[:, None, :]


def softmax_last(logit_rows):
    row_max = jnp.max(logit_rows, axis=-1, keepdims=True)
    exponent = jnp.exp(logit_rows - row_max)
    return exponent / jnp.sum(exponent, axis=-1, keepdims=True)


def build_slots(route_rows, order_rows, expert_ids, capacity):
    length = route_rows.shape[0]
    chosen = route_rows[:, :, None] == expert_ids[None, None, :]
    hit_count = jnp.sum(chosen.astype(jnp.int32), axis=1)
    ordered = hit_count[order_rows]
    before = jnp.cumsum(ordered, axis=0) - ordered
    slot_rank = jnp.zeros_like(before).at[order_rows].set(before)
    kept_mask = (hit_count > 0) & (slot_rank < capacity)
    slot_place = jnp.where(kept_mask, slot_rank, capacity)
    expert_cols = jnp.broadcast_to(
        jnp.arange(expert_ids.shape[0], dtype=jnp.int32)[None, :], slot_place.shape
    )
    token_ids = jnp.broadcast_to(jnp.arange(length, dtype=jnp.int32)[:, None], slot_place.shape)
    table_full = jnp.full((expert_ids.shape[0], capacity + 1), length, jnp.int32)
    table_full = table_full.at[expert_cols, slot_place].set(token_ids)
    return (chosen, table_full[:, :capacity])


def local(
    tokens,
    mixing_weight,
    output_weight,
    norm_gains,
    expert_gate,
    expert_up,
    expert_down,
    gate_logits,
    routes,
    fill_order,
    cotangent,
):
    single = jnp.float32
    narrow = jnp.bfloat16
    groups = lax.axis_size("seq")
    column = lax.axis_index("seq")
    tok_rows = tokens.shape[1]
    seq_len = tok_rows * groups
    capacity = (seq_len * TOP + EXPERTS - 1) // EXPERTS
    local_count = expert_gate.shape[1]
    query_width = HEADS * HEAD_DIM
    key_width = KV_HEADS * HEAD_DIM
    mixing_width = query_width + 2 * key_width
    score_scale = 1.0 / math.sqrt(HEAD_DIM)
    group_size = HEADS // KV_HEADS
    inputs = tokens[0].astype(single)
    mixing_full, exit_full, gains_full = (
        lax.all_gather(mixing_weight, ("seq", "fsdp"), axis=0, tiled=True),
        lax.all_gather(output_weight, ("seq", "fsdp"), axis=0, tiled=True),
        lax.all_gather(norm_gains, ("seq", "fsdp"), axis=0, tiled=True),
    )
    gains_float = gains_full.astype(single)
    normed = norm_apply(inputs, gains_float[:, 0])
    normed_low = normed.astype(narrow)
    projected = jnp.dot(normed_low, mixing_full, preferred_element_type=single)
    positions = column * tok_rows + jnp.arange(tok_rows, dtype=jnp.int32)
    cos_table, sin_table = rotary_tables(positions)
    query_raw = projected[:, :query_width].reshape(tok_rows, HEADS, HEAD_DIM)
    key_raw = projected[:, query_width : query_width + key_width].reshape(
        tok_rows, KV_HEADS, HEAD_DIM
    )
    query_send = (
        rotate(query_raw, cos_table, sin_table).reshape(tok_rows, query_width).astype(narrow)
    )
    key_send = rotate(key_raw, cos_table, sin_table).reshape(tok_rows, key_width).astype(narrow)
    value_send = projected[:, query_width + key_width :].astype(narrow)
    query_heads, key_heads, value_heads = (
        lax.all_to_all(query_send, "seq", split_axis=1, concat_axis=0, tiled=True),
        lax.all_to_all(key_send, "seq", split_axis=1, concat_axis=0, tiled=True),
        lax.all_to_all(value_send, "seq", split_axis=1, concat_axis=0, tiled=True),
    )
    local_kv = key_heads.shape[1] // HEAD_DIM
    blocks = seq_len // QBLK
    query_blocks = query_heads.reshape(blocks, QBLK, local_kv, group_size, HEAD_DIM)
    key_heads = key_heads.reshape(seq_len, local_kv, HEAD_DIM)
    value_heads = value_heads.reshape(seq_len, local_kv, HEAD_DIM)
    starts = jnp.arange(blocks, dtype=jnp.int32) * QBLK
    key_pos = jnp.arange(seq_len, dtype=jnp.int32)

    def block_scores(row_block, first_row):
        scores = (
            jnp.einsum("bkgd,tkd->kgbt", row_block, key_heads, preferred_element_type=single)
            * score_scale
        )
        allowed = (first_row + jnp.arange(QBLK, dtype=jnp.int32))[:, None] >= key_pos[None, :]
        return jnp.where(allowed, scores, -jnp.inf)

    def attend(block_items):
        row_block, first_row = block_items
        scores = block_scores(row_block, first_row)
        row_max = jnp.max(scores, axis=-1, keepdims=True)
        exponent = jnp.exp(scores - row_max)
        row_total = jnp.sum(exponent, axis=-1, keepdims=True)
        soft_weights = (exponent / row_total).astype(narrow)
        attended = jnp.einsum(
            "kgbt,tkd->bkgd", soft_weights, value_heads, preferred_element_type=single
        )
        return (attended.astype(narrow), (row_max + jnp.log(row_total))[..., 0])

    attended_blocks, log_totals = lax.map(attend, (query_blocks, starts))
    attended_heads = attended_blocks.reshape(seq_len, -1)
    attn_rows = lax.all_to_all(attended_heads, "seq", split_axis=0, concat_axis=1, tiled=True)
    attn_out = lax.dot_general(
        attn_rows, exit_full, (((1,), (1,)), ((), ())), preferred_element_type=single
    )
    hidden = inputs + attn_out
    normed_two = norm_apply(hidden, gains_float[:, 1])
    normed_two_low = normed_two.astype(narrow)
    seq_rows = lax.all_gather(normed_two_low, "seq", axis=0, tiled=True)
    expert_ids = column * local_count + jnp.arange(local_count, dtype=jnp.int32)
    gating = softmax_last(gate_logits[0])
    chosen, slot_table = build_slots(routes[0], fill_order[0], expert_ids, capacity)
    chosen_float = chosen.astype(single)
    token_weight = jnp.sum(gating[:, :, None] * chosen_float, axis=1)
    padded_weight = jnp.concatenate([token_weight, jnp.zeros((1, local_count), single)], 0)
    expert_cols = jnp.arange(local_count, dtype=jnp.int32)[:, None]
    slot_weight = padded_weight[slot_table, expert_cols]
    padded_rows = jnp.concatenate([seq_rows, jnp.zeros((1, D), narrow)], 0)
    slot_rows = padded_rows[slot_table]
    gate_full, up_full, down_full = (
        lax.all_gather(expert_gate, "fsdp", axis=0, tiled=True),
        lax.all_gather(expert_up, "fsdp", axis=0, tiled=True),
        lax.all_gather(expert_down, "fsdp", axis=0, tiled=True),
    )
    gate_pre = jnp.einsum("ecd,def->ecf", slot_rows, gate_full, preferred_element_type=single)
    up_pre = jnp.einsum("ecd,def->ecf", slot_rows, up_full, preferred_element_type=single)
    sigmoid_gate = jax.nn.sigmoid(gate_pre)
    mid_low = (gate_pre * sigmoid_gate * up_pre).astype(narrow)
    expert_out = jnp.einsum("ecf,def->ecd", mid_low, down_full, preferred_element_type=single)
    partial_sum = (
        jnp.zeros((seq_len + 1, D), single)
        .at[slot_table]
        .add(expert_out * slot_weight[:, :, None])[:seq_len]
    )
    moe_rows = lax.psum_scatter(
        partial_sum.astype(jnp.bfloat16), "seq", scatter_dimension=0, tiled=True
    ).astype(jnp.float32)
    layer_output = (hidden + moe_rows).astype(narrow)[None]
    cot_rows = lax.all_gather(cotangent[0], "seq", axis=0, tiled=True)
    padded_cot = jnp.concatenate([cot_rows, jnp.zeros((1, D), narrow)], 0)
    slot_cot = padded_cot[slot_table].astype(single)
    slot_weight_grad = jnp.sum(slot_cot * expert_out, axis=-1)
    out_low = (slot_cot * slot_weight[:, :, None]).astype(narrow)
    gate_full, up_full, down_full = (
        lax.all_gather(expert_gate, "fsdp", axis=0, tiled=True),
        lax.all_gather(expert_up, "fsdp", axis=0, tiled=True),
        lax.all_gather(expert_down, "fsdp", axis=0, tiled=True),
    )
    mid_grad = jnp.einsum("ecd,def->ecf", out_low, down_full, preferred_element_type=single)
    gate_grad_low = (
        mid_grad * up_pre * sigmoid_gate * (1.0 + gate_pre * (1.0 - sigmoid_gate))
    ).astype(narrow)
    up_grad_low = (mid_grad * gate_pre * sigmoid_gate).astype(narrow)
    row_grad = jnp.einsum("ecf,def->ecd", gate_grad_low, gate_full, preferred_element_type=single)
    row_grad = row_grad + jnp.einsum(
        "ecf,def->ecd", up_grad_low, up_full, preferred_element_type=single
    )
    normed_two_part = jnp.zeros((seq_len + 1, D), single).at[slot_table].add(row_grad)[:seq_len]
    weight_grad_tok = (
        jnp.zeros((seq_len + 1, local_count), single)
        .at[slot_table, expert_cols]
        .add(slot_weight_grad)[:seq_len]
    )
    route_grad = jnp.sum(weight_grad_tok[:, None, :] * chosen_float, axis=-1)
    logit_part = gating * (route_grad - jnp.sum(gating * route_grad, axis=-1, keepdims=True))
    normed_two_grad, logits_rows = (
        lax.psum_scatter(normed_two_part, "seq", scatter_dimension=0, tiled=True),
        lax.psum_scatter(logit_part, "seq", scatter_dimension=0, tiled=True),
    )
    gate_term = jnp.einsum("ecd,ecf->def", slot_rows, gate_grad_low, preferred_element_type=single)
    up_term = jnp.einsum("ecd,ecf->def", slot_rows, up_grad_low, preferred_element_type=single)
    down_term = jnp.einsum("ecd,ecf->def", out_low, mid_low, preferred_element_type=single)
    expert_total = lax.psum_scatter(
        jnp.concatenate([gate_term, up_term, down_term], 2).astype(jnp.bfloat16),
        "fsdp",
        scatter_dimension=0,
        tiled=True,
    ).astype(jnp.float32)
    unused, norm_two_back = jax.vjp(norm_apply, hidden, gains_float[:, 1])
    hidden_part, gain_two_grad = norm_two_back(normed_two_grad)
    hidden_grad = cotangent[0].astype(single) + hidden_part
    attn_grad_low = hidden_grad.astype(narrow)
    attended_grad = jnp.dot(attn_grad_low, exit_full, preferred_element_type=single).astype(narrow)
    grads_heads = lax.all_to_all(attended_grad, "seq", split_axis=1, concat_axis=0, tiled=True)
    grad_blocks = grads_heads.reshape(blocks, QBLK, local_kv, group_size, HEAD_DIM)

    def attend_back(carried, block_items):
        keys_sum, values_sum = carried
        row_block, grad_block, block_log, first_row = block_items
        scores = block_scores(row_block, first_row)
        soft_float = jnp.exp(scores - block_log[..., None])
        soft_weights = soft_float.astype(narrow)
        values_sum = values_sum + jnp.einsum(
            "kgbt,bkgd->tkd", soft_weights, grad_block, preferred_element_type=single
        )
        soft_grad = jnp.einsum(
            "bkgd,tkd->kgbt", grad_block, value_heads, preferred_element_type=single
        )
        row_delta = jnp.sum(soft_float * soft_grad, axis=-1, keepdims=True)
        scores_grad = (soft_float * (soft_grad - row_delta)).astype(narrow)
        query_grad = (
            jnp.einsum("kgbt,tkd->bkgd", scores_grad, key_heads, preferred_element_type=single)
            * score_scale
        )
        keys_sum = (
            keys_sum
            + jnp.einsum("kgbt,bkgd->tkd", scores_grad, row_block, preferred_element_type=single)
            * score_scale
        )
        return ((keys_sum, values_sum), query_grad.astype(narrow))

    zero_heads = jnp.zeros((seq_len, local_kv, HEAD_DIM), single)
    (keys_sum, values_sum), query_grads = lax.scan(
        attend_back, (zero_heads, zero_heads), (query_blocks, grad_blocks, log_totals, starts)
    )
    query_send_grad = query_grads.reshape(seq_len, -1)
    key_send_grad = keys_sum.reshape(seq_len, -1).astype(narrow)
    value_send_grad = values_sum.reshape(seq_len, -1).astype(narrow)
    query_back, key_back, value_back = (
        lax.all_to_all(query_send_grad, "seq", split_axis=0, concat_axis=1, tiled=True),
        lax.all_to_all(key_send_grad, "seq", split_axis=0, concat_axis=1, tiled=True),
        lax.all_to_all(value_send_grad, "seq", split_axis=0, concat_axis=1, tiled=True),
    )

    def turn_rows(entries):
        return rotate(entries, cos_table, sin_table)

    unused, query_turn_back = jax.vjp(turn_rows, query_raw)
    unused, key_turn_back = jax.vjp(turn_rows, key_raw)
    query_raw_grad = query_turn_back(query_back.astype(single).reshape(tok_rows, HEADS, HEAD_DIM))[
        0
    ]
    key_raw_grad = key_turn_back(key_back.astype(single).reshape(tok_rows, KV_HEADS, HEAD_DIM))[0]
    projected_grad = jnp.concatenate(
        [
            query_raw_grad.reshape(tok_rows, query_width).astype(narrow),
            key_raw_grad.reshape(tok_rows, key_width).astype(narrow),
            value_back,
        ],
        1,
    )
    normed_grad = lax.dot_general(
        projected_grad, mixing_full, (((1,), (1,)), ((), ())), preferred_element_type=single
    )
    unused, norm_one_back = jax.vjp(norm_apply, inputs, gains_float[:, 0])
    input_part, gain_one_grad = norm_one_back(normed_grad)
    tokens_gradient = (hidden_grad + input_part)[None]
    gains_term = jnp.stack([gain_one_grad, gain_two_grad], 1)
    mixing_term = lax.dot_general(
        normed_low, projected_grad, (((0,), (0,)), ((), ())), preferred_element_type=single
    )
    output_term = lax.dot_general(
        attn_grad_low, attn_rows, (((0,), (0,)), ((), ())), preferred_element_type=single
    )
    attn_total = lax.psum_scatter(
        jnp.concatenate([mixing_term, output_term, gains_term], 1),
        ("seq", "fsdp"),
        scatter_dimension=0,
        tiled=True,
    )
    mixing_gradient = attn_total[:, :mixing_width]
    output_gradient = attn_total[:, mixing_width : mixing_width + query_width]
    gains_gradient = attn_total[:, mixing_width + query_width :]
    gate_gradient = expert_total[:, :, :FF]
    up_gradient = expert_total[:, :, FF : 2 * FF]
    down_gradient = expert_total[:, :, 2 * FF :]
    return (
        layer_output,
        tokens_gradient,
        mixing_gradient,
        output_gradient,
        gains_gradient,
        gate_gradient,
        up_gradient,
        down_gradient,
        logits_rows[None],
    )


def solution(mesh):
    in_specs = (
        P("fsdp", "seq", None),
        P(("seq", "fsdp"), None),
        P(("seq", "fsdp"), None),
        P(("seq", "fsdp"), None),
        P("fsdp", "seq", None),
        P("fsdp", "seq", None),
        P("fsdp", "seq", None),
        P("fsdp", None, None),
        P("fsdp", None, None),
        P("fsdp", None),
        P("fsdp", "seq", None),
    )
    out_specs = (
        P("fsdp", "seq", None),
        P("fsdp", "seq", None),
        P(("seq", "fsdp"), None),
        P(("seq", "fsdp"), None),
        P(("seq", "fsdp"), None),
        P("fsdp", "seq", None),
        P("fsdp", "seq", None),
        P("fsdp", "seq", None),
        P("fsdp", "seq", None),
    )
    return jax.shard_map(local, mesh=mesh, in_specs=in_specs, out_specs=out_specs, check_vma=False)
```

profile of v0, /device:TPU:0, one launch (start us, length us, event | category | flops | bytes accessed | tf_op | source)
XLA Modules:
  0.0 1854.2 jit_solution(63584453304176128)
XLA Ops:
  8.7 43.3 %all-gather.1 = bf16[32,48,2]{1,2,0:T(2,128)(2,1)S(1)} all-gather(bf16[1,48,2]{1,2,0:T(2,128)(2,1)} %bitcast.352), channel_id=1, replica_groups=mesh['seq'=4,'fsdp'=8] {'seq','fsdp'}, dimensions={0}, use_global_device_ids=true | all-gather | bytes 6336 | tf_op jit(solution)/shard_map/all_gather | solution.py:94
  57.3 32.0 %all-gather.10.cloned.1.call-done = bf16[1536,2560]{1,0:T(8,128)(2,1)} async-done(((bf16[48,2560]{1,0:T(8,128)(2,1)}), bf16[1536,2560]{1,0:T(8,128)(2,1)}) %all-gather.10.cloned.1.call-update) | async-done | bytes 7864336 | tf_op jit(solution)/shard_map/all_gather | solution.py:92
  131.2 12.9 all-to-all-done
  147.4 23.8 %while.28 = (s32[]{:T(128)}, bf16[2,512,2,3,64]{1,4,3,2,0:T(8,128)(2,1)S(1)}, f32[2,2,3,512]{3,2,1,0:T(4,128)S(1)}, s32[2]{0:T(128)S(1)}, bf16[2,512,2,3,64]{1,4...) while((s32[]{:T(128)}, ...), condition=%wide.region_4.5_spmd.clone, body=%wide.region_1.4_spmd.clone.sunk | while | flops 843773440 | bytes 41279608 | solution.py:144
  180.1 12.1 all-to-all-done.3
  213.5 37.9 %scatter_custom_fusion.3 = s32[2060]{0:T(1024)S(1)} fusion(s32[10240]{0:T(1024)S(1)} %reshape.356, s32[10240]{0:T(1024)S(1)} %reshape.358, s32[]{:T(128)} %constant.52.clone.1), kind=kCustom, calls=%fused_computation.179 | custom fusion | bytes 8244
  254.8 8.5 gather_fusion.3
  263.3 11.4 reshape.378
  276.8 8.5 gather_fusion.1
  285.3 8.8 reshape.311
  294.1 101.2 %all-gather.16.cloned.1.call-done = bf16[1536,10,512]{2,0,1:T(8,128)(2,1)} async-done(((bf16[192,10,512]{2,0,1:T(8,128)(2,1)}), bf16[1536,10,512]{2,0,1:T(8,128)(2,1)}) %all-gather.16.cloned.1.call-update) | async-done | bytes 15728656 | tf_op jit(solution)/shard_map/all_gather | solution.py:165
  395.3 13.3 fusion.103
  408.6 128.9 %all-gather.18.cloned.1.call-done = bf16[1536,10,512]{2,0,1:T(8,128)(2,1)} async-done(((bf16[192,10,512]{2,0,1:T(8,128)(2,1)}), bf16[1536,10,512]{2,0,1:T(8,128)(2,1)}) %all-gather.18.cloned.1.call-update) | async-done | bytes 15728656 | tf_op jit(solution)/shard_map/all_gather | solution.py:166
  537.5 15.1 multiply_convert_fusion.3
  552.6 127.2 %all-gather.20.cloned.1.call-done = bf16[1536,10,512]{2,0,1:T(8,128)(2,1)} async-done(((bf16[192,10,512]{2,0,1:T(8,128)(2,1)}), bf16[1536,10,512]{2,0,1:T(8,128)(2,1)}) %all-gather.20.cloned.1.call-update) | async-done | bytes 15728656 | tf_op jit(solution)/shard_map/all_gather | solution.py:167
  679.8 15.5 multiply_reduce_fusion
  695.4 16.0 scatter_custom_fusion.4
  712.6 19.8 %gather_fusion.2 = f32[2050]{0:T(1024)S(1)} fusion(f32[1025,10]{1,0:T(8,128)S(1)} %concatenate.44, s32[2050]{0:T(1024)S(1)} %reshape.318), kind=kCustom, calls=%fused_computation.2 | custom fusion | bytes 32800 | tf_op jit(solution)/shard_map/gather | solution.py:161
  732.5 15.0 multiply_convert_fusion.1
  747.5 12.8 fusion.104
  760.3 15.0 convolution_add_fusion
  775.3 12.5 reshape.352
  787.8 29.5 %scatter_custom_fusion.2 = f32[1025,1536]{1,0:T(8,128)} fusion(s32[2050]{0:T(1024)S(1)} %reshape.342, f32[2050,1536]{1,0:T(8,128)} %reshape.352, f32[]{:T(128)} %constant.30.clone.1), kind=kCustom, calls=%fused_computation.87 | custom fusion | flops 3148800 | bytes 6298112 | tf_op jit(solution)/shard_map/scatter-add | solution.py:202
  817.4 5.9 slice.109
  823.4 10.2 broadcast_multiply_fusion
  833.5 13.2 reshape.344
  846.7 29.4 %scatter_custom_fusion.1 = f32[1025,1536]{1,0:T(8,128)} fusion(s32[2050]{0:T(1024)S(1)} %reshape.342, f32[2050,1536]{1,0:T(8,128)} %reshape.344, f32[]{:T(128)} %constant.30.clone.1), kind=kCustom, calls=%fused_computation.89 | custom fusion | flops 3148800 | bytes 6298112 | tf_op jit(solution)/shard_map/scatter-add | solution.py:177
  881.1 10.8 reduce-scatter.10.cloned.1.call-done
  894.3 45.2 %reduce-scatter.8.cloned.1.call-done = bf16[256,1536]{1,0:T(8,128)(2,1)} async-done(((bf16[1024,1536]{1,0:T(8,128)(2,1)}), bf16[256,1536]{1,0:T(8,128)(2,1)}) %reduce-scatter.8.cloned.1.call-update) | async-done | bytes 786448 | tf_op jit(solution)/shard_map/reduce_scatter | solution.py:179
  952.3 11.0 all-to-all-done.4
  966.4 56.4 %while.29 = (s32[]{:T(128)}, f32[1024,2,64]{0,2,1:T(8,128)S(1)}, f32[1024,2,64]{0,2,1:T(8,128)}, bf16[2,512,2,3,64]{1,4,3,2,0:T(8,128)(2,1)}, bf16[2,512,2,3,64]...) while((s32[]{:T(128)}, f32[1024,2,64]{0,2,1:T(8,128)S(1)}, ...), condition=%wide.region_21.22_spmd.clone, body=%wide.region_19.21_spmd.clone.sunk | while | flops 2062022144 | bytes 184250800 | solution.py:257
  970.0 5.7 fusion.160
  985.0 6.6 fusion.163
  1013.2 6.6 fusion.163
  1027.4 6.7 fusion.75
  1042.8 9.5 all-to-all-done.5
  1061.1 7.9 fusion.72
  1069.0 6.8 fusion.65
  1076.1 27.7 %concatenate.48 = f32[1536,4098]{1,0:T(8,128)} concatenate(f32[1536,2560]{1,0:T(8,128)} %fusion.72, f32[1536,1536]{1,0:T(8,128)} %fusion.75, f32[1536,1]{1,0:T(8,128)S(1)} %stack.8, f32[1536,1]{1,0:T(8,128)S(1)} %copy-done.25), dimensions={1} | concatenate | bytes 50356224 | tf_op jit(solution)/shard_map/concatenate | solution.py:300
  1105.4 12.4 convert_bitcast_fusion.1
  1117.8 12.8 convert_bitcast_fusion.2
  1130.6 15.1 convert_bitcast_fusion
  1145.7 35.1 %pad_maximum_fusion = bf16[1536,10,1536]{0,2,1:T(8,128)(2,1)} fusion(bf16[1536,10,512]{0,2,1:T(8,128)(2,1)} %convert_bitcast_fusion, bf16[1536,10,512]{0,2,1:T(8,128)(2,1)} %convert_bitcast_fusion.1, bf16[1536,10,512]{0,2,1:T(8,128)(2,1)} %convert_bitcast_fusion.2), kind=kLoop, calls=%fused_computation.74 | loop fusion | flops 141557760 | bytes 94371840 | tf_op jit(solution)/shard_map/concatenate | solution.py:218
  1180.8 57.6 %copy.314 = bf16[1536,15360]{1,0:T(8,128)(2,1)} copy(bf16[1536,15360]{0,1:T(8,128)(2,1)} %bitcast.320) | data formatting | bytes 94371840
  1242.9 112.8 %reduce-scatter.12.cloned.1.call-done = f32[48,4098]{1,0:T(8,128)} async-done(((f32[1536,4098]{1,0:T(8,128)}), f32[48,4098]{1,0:T(8,128)}) %reduce-scatter.12.cloned.1.call-update) | async-done | bytes 786832 | tf_op jit(solution)/shard_map/reduce_scatter | solution.py:299
  1360.7 450.7 %reduce-scatter.16.cloned.1.call-done = bf16[192,15360]{1,0:T(8,128)(2,1)} async-done(((bf16[1536,15360]{1,0:T(8,128)(2,1)}), bf16[192,15360]{1,0:T(8,128)(2,1)}) %reduce-scatter.16.cloned.1.call-update) | async-done | bytes 5898256
  1811.3 9.7 copy.315
  1821.0 9.3 fusion.100
  (362 shorter events, 222.0 us)
Async XLA Ops:
  7.2 49.8 %copy-start.17 = (bf16[1,256,1536]{2,1,0:T(8,128)(2,1)S(1)}, bf16[1,256,1536]{2,1,0:T(8,128)(2,1)}, u32[]{:S(2)}) copy-start(bf16[1,256,1536]{2,1,0:T(8,128)(2,1)} %param.15) | copy-start | bytes 2359300
  7.2 82.1 %all-gather.10.cloned.1.call-start = ((), (), s32[]{:S(2)}) async-start(), calls=%async_computation.13 | async-start | bytes 8110080 | tf_op jit(solution)/shard_map/all_gather | solution.py:92
  7.9 172.2 %all-gather.12.cloned.1.call-start = ((), (), s32[]{:S(2)}) async-start(), calls=%async_computation.14 | async-start | bytes 4866048 | tf_op jit(solution)/shard_map/all_gather | solution.py:93
  52.3 42.5 %copy-start.26 = (f32[256,64]{0,1:T(8,128)}, f32[256,64]{0,1:T(8,128)S(1)}, u32[]{:S(2)}) copy-start(f32[256,64]{0,1:T(8,128)S(1)} %get-tuple-element.430) | copy-start | bytes 196612
  52.3 53.7 %copy-start.28 = (f32[256,64]{0,1:T(8,128)}, f32[256,64]{0,1:T(8,128)S(1)}, u32[]{:S(2)}) copy-start(f32[256,64]{0,1:T(8,128)S(1)} %get-tuple-element.431) | copy-start | bytes 196612
  57.0 37.8 %copy-start.36 = (f32[1536]{0:T(1024)}, f32[1536]{0:T(1024)S(1)}, u32[]{:S(2)}) copy-start(f32[1536]{0:T(1024)S(1)} %get-tuple-element.365) | copy-start | bytes 18436
  57.0 140.0 %copy-start.42 = (f32[1536]{0:T(1024)}, f32[1536]{0:T(1024)S(1)}, u32[]{:S(2)}) copy-start(f32[1536]{0:T(1024)S(1)} %get-tuple-element.364) | copy-start | bytes 18436
  57.2 37.6 %copy-start.54 = (f32[256]{0:T(256)}, f32[256]{0:T(256)S(1)}, u32[]{:S(2)}) copy-start(f32[256]{0:T(256)S(1)} %fusion.69) | copy-start | bytes 3076
  57.2 37.6 %copy-start.50 = (f32[256]{0:T(256)}, f32[256]{0:T(256)S(1)}, u32[]{:S(2)}) copy-start(f32[256]{0:T(256)S(1)} %fusion.95) | copy-start | bytes 3076
  108.1 9.4 all-to-all-start.1
  117.5 8.8 all-to-all-start.2
  126.2 17.9 all-to-all-start
  129.7 122.4 %all-gather.22.cloned.1.call-start = ((), (), s32[]{:S(2)}) async-start(), calls=%async_computation.23 | async-start | bytes 3932160 | tf_op jit(solution)/shard_map/all_gather | solution.py:183
  171.2 25.2 %copy-start.1 = (bf16[1024,2,64]{0,2,1:T(8,128)(2,1)}, bf16[1024,2,64]{0,2,1:T(8,128)(2,1)S(1)}, u32[]{:S(2)}) copy-start(bf16[1024,2,64]{0,2,1:T(8,128)(2,1)S(1)} %get-tuple-element.621) | copy-start | bytes 786436
  171.2 25.2 %copy-start.3 = (bf16[2,512,2,3,64]{1,4,3,2,0:T(8,128)(2,1)}, bf16[2,512,2,3,64]{1,4,3,2,0:T(8,128)(2,1)S(1)}, u32[]{:S(2)}) copy-start(bf16[2,512,2,3,64]{1,4,3,2,0:T(8,128)(2,1)S(1)} %get-tuple-element.622) | copy-start | bytes 2359300
  171.2 25.2 %copy-start.16 = (bf16[1024,2,64]{0,2,1:T(8,128)(2,1)}, bf16[1024,2,64]{0,2,1:T(8,128)(2,1)S(1)}, u32[]{:S(2)}) copy-start(bf16[1024,2,64]{0,2,1:T(8,128)(2,1)S(1)} %get-tuple-element.629) | copy-start | bytes 786436
  171.2 25.2 %copy-start.38 = (f32[2,2,3,512]{3,2,1,0:T(4,128)}, f32[2,2,3,512]{3,2,1,0:T(4,128)S(1)}, u32[]{:S(2)}) copy-start(f32[2,2,3,512]{3,2,1,0:T(4,128)S(1)} %get-tuple-element.575) | copy-start | bytes 73732
  171.2 25.2 %copy-start.63 = (s32[2]{0:T(128)}, s32[2]{0:T(128)S(1)}, u32[]{:S(2)}) copy-start(s32[2]{0:T(128)S(1)} %get-tuple-element.663) | copy-start | bytes 28
  176.5 15.7 all-to-all-start.3
  180.0 94.7 %all-gather.14.cloned.1.call-start = ((), (), s32[]{:S(2)}) async-start(), calls=%async_computation.15 | async-start | bytes 3932160 | tf_op jit(solution)/shard_map/all_gather | solution.py:153
  198.7 196.6 %all-gather.16.cloned.1.call-start = ((), (), s32[]{:S(2)}) async-start(), calls=%async_computation.16 | async-start | bytes 17694720 | tf_op jit(solution)/shard_map/all_gather | solution.py:165
  199.3 338.2 %all-gather.18.cloned.1.call-start = ((), (), s32[]{:S(2)}) async-start(), calls=%async_computation.17 | async-start | bytes 17694720 | tf_op jit(solution)/shard_map/all_gather | solution.py:166
  199.8 480.0 %all-gather.20.cloned.1.call-start = ((), (), s32[]{:S(2)}) async-start(), calls=%async_computation.18 | async-start | bytes 17694720 | tf_op jit(solution)/shard_map/all_gather | solution.py:167
  200.6 691.3 %reduce-scatter.10.cloned.1.call-start = ((), (), s32[]{:S(2)}) async-start(), calls=%async_computation.20 | async-start | bytes 7864320 | tf_op jit(solution)/shard_map/reduce_scatter | solution.py:211
  204.4 47.2 %copy-start.60 = (s32[2]{0:T(128)S(1)}, s32[2]{0:T(128)}, u32[]{:S(2)}) copy-start(s32[2]{0:T(128)} %constant.133) | copy-start | bytes 28
  204.4 47.3 %copy-start.59 = (s32[2]{0:T(128)S(1)}, s32[2]{0:T(128)}, u32[]{:S(2)}) copy-start(s32[2]{0:T(128)} %constant.136) | copy-start | bytes 28
  204.4 47.6 %copy-start.30 = (f32[1,1024,8]{1,2,0:T(8,128)S(1)}, f32[1,1024,8]{1,2,0:T(8,128)}, u32[]{:S(2)}) copy-start(f32[1,1024,8]{1,2,0:T(8,128)} %param.22) | copy-start | bytes 98308
  552.6 142.8 %copy-start.5 = (bf16[10,205,512]{2,1,0:T(8,128)(2,1)}, bf16[10,205,512]{2,1,0:T(8,128)(2,1)S(1)}, u32[]{:S(2)}) copy-start(bf16[10,205,512]{2,1,0:T(8,128)(2,1)S(1)} %get-tuple-element.425) | copy-start | bytes 6297604
  732.5 90.9 %copy-start.40 = (f32[10,205]{1,0:T(8,128)}, f32[10,205]{1,0:T(8,128)S(1)}, u32[]{:S(2)}) copy-start(f32[10,205]{1,0:T(8,128)S(1)} %reshape.321) | copy-start | bytes 24604
  823.3 116.2 %reduce-scatter.8.cloned.1.call-start = ((), (), s32[]{:S(2)}) async-start(), calls=%async_computation.19 | async-start | bytes 3932160 | tf_op jit(solution)/shard_map/reduce_scatter | solution.py:179
  876.2 15.8 copy-start.14
  876.2 15.8 copy-start.43
  876.2 15.8 copy-start.53
  881.1 13.2 copy-start.57
  881.1 58.4 %copy-start.20 = (bf16[1,256,1536]{2,1,0:T(8,128)(2,1)S(1)}, bf16[1,256,1536]{2,1,0:T(8,128)(2,1)}, u32[]{:S(2)}) copy-start(bf16[1,256,1536]{2,1,0:T(8,128)(2,1)} %param.25) | copy-start | bytes 2359300
  947.4 19.0 %copy-start.2 = (bf16[1024,2,64]{0,2,1:T(8,128)(2,1)S(1)}, bf16[1024,2,64]{0,2,1:T(8,128)(2,1)}, u32[]{:S(2)}) copy-start(bf16[1024,2,64]{0,2,1:T(8,128)(2,1)} %copy-done.1) | copy-start | bytes 786436
  947.4 19.0 %copy-start.4 = (bf16[2,512,2,3,64]{1,4,3,2,0:T(8,128)(2,1)S(1)}, bf16[2,512,2,3,64]{1,4,3,2,0:T(8,128)(2,1)}, u32[]{:S(2)}) copy-start(bf16[2,512,2,3,64]{1,4,3,2,0:T(8,128)(2,1)} %copy-done.3) | copy-start | bytes 2359300
  947.4 19.0 %copy-start.39 = (f32[2,2,3,512]{3,2,1,0:T(4,128)S(1)}, f32[2,2,3,512]{3,2,1,0:T(4,128)}, u32[]{:S(2)}) copy-start(f32[2,2,3,512]{3,2,1,0:T(4,128)} %copy-done.38) | copy-start | bytes 73732
  947.4 19.0 %copy-start.64 = (s32[2]{0:T(128)S(1)}, s32[2]{0:T(128)}, u32[]{:S(2)}) copy-start(s32[2]{0:T(128)} %copy-done.63) | copy-start | bytes 28
  948.6 14.7 all-to-all-start.4
  1023.7 14.7 all-to-all-start.6
  1038.4 14.0 all-to-all-start.5
  1052.4 8.8 all-to-all-start.7
  1055.8 300.0 %reduce-scatter.12.cloned.1.call-start = ((), (), s32[]{:S(2)}) async-start(), calls=%async_computation.21 | async-start | bytes 26763264 | tf_op jit(solution)/shard_map/reduce_scatter | solution.py:299
  1103.8 707.6 %reduce-scatter.16.cloned.1.call-start = ((), (), s32[]{:S(2)}) async-start(), calls=%async_computation.24 | async-start | bytes 53084160
  1117.7 12.8 copy-start.6
  1117.7 12.8 copy-start.41
  1238.4 608.5 %reduce-scatter.14.cloned.1.call-start = ((), (), s32[]{:S(2)}) async-start(), calls=%async_computation.22 | async-start | bytes 40960 | tf_op jit(solution)/shard_map/reduce_scatter | solution.py:212
  (48 other events, 239.1 us)
Sparse Core Ops, SparseCore 0:
  11.0 78.1 all-gather.9
  92.3 64.7 all-gather.11
  158.9 46.2 all-gather.21
  207.5 43.7 all-gather.13
  252.7 142.5 all-gather.15
  396.7 140.6 all-gather.17
  539.1 140.6 all-gather.19
  823.4 68.4 reduce-scatter.9
  895.5 43.9 reduce-scatter.7
  1103.9 251.8 reduce-scatter.11
  1358.1 453.1 reduce-scatter.15
  1814.5 21.9 reduce-scatter.13
where the time goes:
time: 1860 us; the launch traced here: 1850 us
  waiting for transfers between devices  1070 us (58%)
  local copies, waits for them, and re-layouts  315 us (17%)
  matrix products  216 us (12%)
  other arithmetic  165 us (9%)
  blocking collectives  43.3 us (2%)
  starting transfers between devices  29.8 us (2%)
    unnamed x13, waiting for transfers between devices  454 us
    unnamed x131, local copies, waits for them, and re-layouts  131 us
    all_gather x1, waiting for transfers between devices, local(): lax.all_gather(expert_up, 'fsdp', axis=0, tiled=True)  129 us
    all_gather x1, waiting for transfers between devices, local(): lax.all_gather(expert_down, 'fsdp', axis=0, tiled=True)  127 us
    reduce_scatter x1, waiting for transfers between devices, local(): lax.psum_scatter(jnp.concatenate([mixing_term, output_term, gains_term],...  113 us
    all_gather x1, waiting for transfers between devices, local(): lax.all_gather(expert_gate, 'fsdp', axis=0, tiled=True)  101 us
    reduce_scatter x1, waiting for transfers between devices, local(): lax.psum_scatter(partial_sum.astype(jnp.bfloat16), 'seq', scatter_dimensi...  45.2 us
    all_gather x1, blocking collectives, local(): lax.all_gather(norm_gains, ('seq', 'fsdp'), axis=0, tiled=True)  43.3 us
  transfers between devices with their start and end apart: 20, of which 15 were waited for; matrix products, arithmetic and copies ran while one was open for 23% of the time, Pallas kernels for 0%

commit v1 on v0

--- a/solution.py
+++ b/solution.py
@@ -14,6 +14,25 @@
 QBLK = 512
 epsilon = 1e-05
 rope_base = 10000.0
+
+
+def _define_gates(sheet, along_dim):
+    y = list(sheet.shape[1:])
+    y[along_dim] *= sheet.shape[0]
+    return jnp.moveaxis(sheet, 0, along_dim).reshape(y)
+
+
+def advance_node(arr_in, chip_axis):
+    w1, upper = (lax.axis_size(chip_axis), lax.axis_index(chip_axis))
+    current_value, latest = (arr_in[None], 1)
+    while latest < w1:
+        w2 = lax.ppermute(current_value, chip_axis, [(s, s ^ latest) for s in range(w1)])
+        tall = upper & latest == 0
+        current_value = jnp.concatenate(
+            [jnp.where(tall, current_value, w2), jnp.where(tall, w2, current_value)]
+        )
+        latest *= 2
+    return current_value
 
 
 def norm_apply(values, gain_row):
@@ -161,8 +180,12 @@
     slot_weight = padded_weight[slot_table, expert_cols]
     padded_rows = jnp.concatenate([seq_rows, jnp.zeros((1, D), narrow)], 0)
     slot_rows = padded_rows[slot_table]
+
+    def surface_pack(vector, x_part, dimension_no):
+        return _define_gates(advance_node(vector, x_part), dimension_no)
+
     gate_full, up_full, down_full = (
-        lax.all_gather(expert_gate, "fsdp", axis=0, tiled=True),
+        surface_pack(expert_gate, "fsdp", 0),
         lax.all_gather(expert_up, "fsdp", axis=0, tiled=True),
         lax.all_gather(expert_down, "fsdp", axis=0, tiled=True),
     )

time: 1860 us -> 2250 us (1.21)
  waiting for transfers between devices: 1070 us -> 1420 us
  other arithmetic: 165 us -> 191 us
    ppermute x0 -> x3, waiting for transfers between devices: none -> 713 us  [advance_node(): lax.ppermute(current_value, chip_axis, [(s, s ^ latest) for s in range(w1)])]
    all_gather x1, waiting for transfers between devices: 129 us -> 0.01 us  [local(): lax.all_gather(expert_up, 'fsdp', axis=0, tiled=True)]
    all_gather x1, waiting for transfers between devices: 127 us -> 0.01 us  [local(): lax.all_gather(expert_down, 'fsdp', axis=0, tiled=True)]
    all_gather x1, waiting for transfers between devices: 101 us -> 0.01 us  [local(): lax.all_gather(expert_gate, 'fsdp', axis=0, tiled=True)]
    unnamed x131 -> x135, local copies, waits for them, and re-layouts: 131 us -> 133 us
  transfers between devices with their start and end apart: 20 -> 23, of which waited for: 15 -> 15; matrix products, arithmetic and copies ran while one was open for 23% -> 24% of each run, Pallas kernels for 0% -> 0%
where the time goes in v1:
time: 2250 us; the launch traced here: 2240 us
  waiting for transfers between devices  1420 us (63%)
  local copies, waits for them, and re-layouts  322 us (14%)
  matrix products  216 us (10%)
  other arithmetic  191 us (8%)
  blocking collectives  43.3 us (2%)
  starting transfers between devices  31.1 us (1%)
    ppermute x3, waiting for transfers between devices, advance_node(): lax.ppermute(current_value, chip_axis, [(s, s ^ latest) for s in range(w1)])  713 us
    unnamed x13, waiting for transfers between devices  454 us
    unnamed x135, local copies, waits for them, and re-layouts  133 us
    reduce_scatter x1, waiting for transfers between devices, local(): lax.psum_scatter(jnp.concatenate([mixing_term, output_term, gains_term],...  113 us
    reduce_scatter x1, waiting for transfers between devices, local(): lax.psum_scatter(partial_sum.astype(jnp.bfloat16), 'seq', scatter_dimensi...  45.2 us
  transfers between devices with their start and end apart: 23, of which 15 were waited for; matrix products, arithmetic and copies ran while one was open for 24% of the time, Pallas kernels for 0%

profile of v1, /device:TPU:0, one launch (start us, length us, event | category | flops | bytes accessed | tf_op | source)
XLA Modules:
  0.0 2244.1 jit_solution(1385385401761655952)
XLA Ops:
  8.7 43.3 %all-gather.1 = bf16[32,48,2]{1,2,0:T(2,128)(2,1)S(1)} all-gather(bf16[1,48,2]{1,2,0:T(2,128)(2,1)} %bitcast.358), channel_id=1, replica_groups=mesh['seq'=4,'fsdp'=8] {'seq','fsdp'}, dimensions={0}, use_global_device_ids=true | all-gather | bytes 6336 | tf_op jit(solution)/shard_map/all_gather | solution.py:113
  57.3 32.0 %all-gather.10.cloned.1.call-done = bf16[1536,2560]{1,0:T(8,128)(2,1)} async-done(((bf16[48,2560]{1,0:T(8,128)(2,1)}), bf16[1536,2560]{1,0:T(8,128)(2,1)}) %all-gather.10.cloned.1.call-update) | async-done | bytes 7864336 | tf_op jit(solution)/shard_map/all_gather | solution.py:111
  131.2 12.9 all-to-all-done
  147.5 23.8 %while.28 = (s32[]{:T(128)}, bf16[2,512,2,3,64]{1,4,3,2,0:T(8,128)(2,1)S(1)}, f32[2,2,3,512]{3,2,1,0:T(4,128)S(1)}, s32[2]{0:T(128)S(1)}, bf16[2,512,2,3,64]{1,4...) while((s32[]{:T(128)}, ...), condition=%wide.region_4.5_spmd.clone, body=%wide.region_1.4_spmd.clone.sunk | while | flops 843773440 | bytes 41279608 | solution.py:163
  180.2 12.3 all-to-all-done.3
  211.7 185.0 %collective-permute-done.1 = bf16[2,192,10,512]{3,1,2,0:T(8,128)(2,1)} collective-permute-done((bf16[2,192,10,512]{3,1,2,0:T(8,128)(2,1)}, bf16[2,192,10,512]{3,1,2,0:T(8,128)(2,1)}, u32[]{:S(2)}, u32[]{:S(2)}) %collective-permute-start.1) | collective-permute-done | bytes 3932192 | tf_op jit(solution)/shard_map/ppermute | solution.py:29
  401.9 7.2 pad_maximum_fusion.2
  422.1 38.1 %scatter_custom_fusion.3 = s32[2060]{0:T(1024)S(1)} fusion(s32[10240]{0:T(1024)S(1)} %reshape.360, s32[10240]{0:T(1024)S(1)} %reshape.362, s32[]{:T(128)} %constant.56.clone.1), kind=kCustom, calls=%fused_computation.188 | custom fusion | bytes 8244
  463.6 8.4 gather_fusion.3
  472.1 10.5 reshape.382
  482.6 523.5 %collective-permute-done.2 = bf16[4,192,10,512]{3,1,2,0:T(8,128)(2,1)} collective-permute-done((bf16[4,192,10,512]{3,1,2,0:T(8,128)(2,1)}, bf16[4,192,10,512]{3,1,2,0:T(8,128)(2,1)}, u32[]{:S(2)}, u32[]{:S(2)}) %collective-permute-start.2) | collective-permute-done | bytes 7864352 | tf_op jit(solution)/shard_map/ppermute | solution.py:29
  1006.1 6.1 broadcast_select_fusion.1
  1013.7 6.4 copy.293
  1022.2 8.5 gather_fusion.1
  1030.7 8.9 reshape.315
  1039.5 12.9 fusion.103
  1052.5 14.1 multiply_convert_fusion.3
  1066.6 16.3 multiply_reduce_fusion
  1083.0 16.0 scatter_custom_fusion.4
  1100.2 19.8 gather_fusion.2
  1120.1 15.9 multiply_convert_fusion.1
  1135.9 11.8 fusion.104
  1147.7 16.0 convolution_add_fusion
  1163.7 12.6 reshape.356
  1176.3 29.9 %scatter_custom_fusion.2 = f32[1025,1536]{1,0:T(8,128)} fusion(s32[2050]{0:T(1024)} %copy-done.50, f32[2050,1536]{1,0:T(8,128)} %reshape.356, f32[]{:T(128)} %constant.31.clone.1), kind=kCustom, calls=%fused_computation.94 | custom fusion | flops 3148800 | bytes 6298112 | tf_op jit(solution)/shard_map/scatter-add | solution.py:225
  1212.2 10.2 broadcast_multiply_fusion
  1222.4 12.8 reshape.348
  1235.2 29.5 %scatter_custom_fusion.1 = f32[1025,1536]{1,0:T(8,128)} fusion(s32[2050]{0:T(1024)} %copy-done.50, f32[2050,1536]{1,0:T(8,128)} %reshape.348, f32[]{:T(128)} %constant.31.clone.1), kind=kCustom, calls=%fused_computation.96 | custom fusion | flops 3148800 | bytes 6298112 | tf_op jit(solution)/shard_map/scatter-add | solution.py:200
  1269.6 11.9 reduce-scatter.10.cloned.1.call-done
  1283.9 45.2 %reduce-scatter.8.cloned.1.call-done = bf16[256,1536]{1,0:T(8,128)(2,1)} async-done(((bf16[1024,1536]{1,0:T(8,128)(2,1)}), bf16[256,1536]{1,0:T(8,128)(2,1)}) %reduce-scatter.8.cloned.1.call-update) | async-done | bytes 786448 | tf_op jit(solution)/shard_map/reduce_scatter | solution.py:202
  1341.9 11.0 all-to-all-done.4
  1355.9 56.5 %while.29 = (s32[]{:T(128)}, f32[1024,2,64]{0,2,1:T(8,128)S(1)}, f32[1024,2,64]{0,2,1:T(8,128)}, bf16[2,512,2,3,64]{1,4,3,2,0:T(8,128)(2,1)}, bf16[2,512,2,3,64]...) while((s32[]{:T(128)}, f32[1024,2,64]{0,2,1:T(8,128)S(1)}, ...), condition=%wide.region_21.22_spmd.clone, body=%wide.region_19.21_spmd.clone.sunk | while | flops 2062022144 | bytes 184250800 | solution.py:280
  1374.6 6.6 fusion.163
  1402.9 6.6 fusion.163
  1417.2 6.9 fusion.75
  1432.8 9.5 all-to-all-done.5
  1451.1 7.9 fusion.72
  1459.0 6.8 fusion.65
  1466.0 27.7 %concatenate.60 = f32[1536,4098]{1,0:T(8,128)} concatenate(f32[1536,2560]{1,0:T(8,128)} %fusion.72, f32[1536,1536]{1,0:T(8,128)} %fusion.75, f32[1536,1]{1,0:T(8,128)S(1)} %stack.8, f32[1536,1]{1,0:T(8,128)S(1)} %copy-done.26), dimensions={1} | concatenate | bytes 50356224 | tf_op jit(solution)/shard_map/concatenate | solution.py:323
  1495.3 12.3 convert_bitcast_fusion.1
  1507.6 12.8 convert_bitcast_fusion.2
  1520.4 15.1 convert_bitcast_fusion
  1535.5 35.6 %pad_maximum_fusion = bf16[1536,10,1536]{0,2,1:T(8,128)(2,1)} fusion(bf16[1536,10,512]{0,2,1:T(8,128)(2,1)} %convert_bitcast_fusion, bf16[1536,10,512]{0,2,1:T(8,128)(2,1)} %convert_bitcast_fusion.1, bf16[1536,10,512]{0,2,1:T(8,128)(2,1)} %convert_bitcast_fusion.2), kind=kLoop, calls=%fused_computation.74 | loop fusion | flops 141557760 | bytes 94371840 | tf_op jit(solution)/shard_map/concatenate | solution.py:241
  1571.1 57.5 %copy.322 = bf16[1536,15360]{1,0:T(8,128)(2,1)} copy(bf16[1536,15360]{0,1:T(8,128)(2,1)} %bitcast.324) | data formatting | bytes 94371840
  1633.1 112.8 %reduce-scatter.12.cloned.1.call-done = f32[48,4098]{1,0:T(8,128)} async-done(((f32[1536,4098]{1,0:T(8,128)}), f32[48,4098]{1,0:T(8,128)}) %reduce-scatter.12.cloned.1.call-update) | async-done | bytes 786832 | tf_op jit(solution)/shard_map/reduce_scatter | solution.py:322
  1750.8 450.7 %reduce-scatter.16.cloned.1.call-done = bf16[192,15360]{1,0:T(8,128)(2,1)} async-done(((bf16[1536,15360]{1,0:T(8,128)(2,1)}), bf16[192,15360]{1,0:T(8,128)(2,1)}) %reduce-scatter.16.cloned.1.call-update) | async-done | bytes 5898256
  2201.5 9.7 copy.323
  2211.2 9.3 fusion.100
  (379 shorter events, 251.5 us)
Async XLA Ops:
  7.2 49.8 %copy-start.17 = (bf16[1,256,1536]{2,1,0:T(8,128)(2,1)S(1)}, bf16[1,256,1536]{2,1,0:T(8,128)(2,1)}, u32[]{:S(2)}) copy-start(bf16[1,256,1536]{2,1,0:T(8,128)(2,1)} %param.15) | copy-start | bytes 2359300
  7.2 82.1 %all-gather.10.cloned.1.call-start = ((), (), s32[]{:S(2)}) async-start(), calls=%async_computation.13 | async-start | bytes 8110080 | tf_op jit(solution)/shard_map/all_gather | solution.py:111
  7.9 172.3 %all-gather.12.cloned.1.call-start = ((), (), s32[]{:S(2)}) async-start(), calls=%async_computation.14 | async-start | bytes 4866048 | tf_op jit(solution)/shard_map/all_gather | solution.py:112
  52.3 42.5 %copy-start.27 = (f32[256,64]{0,1:T(8,128)}, f32[256,64]{0,1:T(8,128)S(1)}, u32[]{:S(2)}) copy-start(f32[256,64]{0,1:T(8,128)S(1)} %get-tuple-element.436) | copy-start | bytes 196612
  52.3 53.6 %copy-start.29 = (f32[256,64]{0,1:T(8,128)}, f32[256,64]{0,1:T(8,128)S(1)}, u32[]{:S(2)}) copy-start(f32[256,64]{0,1:T(8,128)S(1)} %get-tuple-element.437) | copy-start | bytes 196612
  57.0 37.8 %copy-start.37 = (f32[1536]{0:T(1024)}, f32[1536]{0:T(1024)S(1)}, u32[]{:S(2)}) copy-start(f32[1536]{0:T(1024)S(1)} %get-tuple-element.365) | copy-start | bytes 18436
  57.0 140.2 %copy-start.43 = (f32[1536]{0:T(1024)}, f32[1536]{0:T(1024)S(1)}, u32[]{:S(2)}) copy-start(f32[1536]{0:T(1024)S(1)} %get-tuple-element.364) | copy-start | bytes 18436
  57.2 37.6 %copy-start.56 = (f32[256]{0:T(256)}, f32[256]{0:T(256)S(1)}, u32[]{:S(2)}) copy-start(f32[256]{0:T(256)S(1)} %fusion.69) | copy-start | bytes 3076
  57.2 37.6 %copy-start.52 = (f32[256]{0:T(256)}, f32[256]{0:T(256)S(1)}, u32[]{:S(2)}) copy-start(f32[256]{0:T(256)S(1)} %fusion.95) | copy-start | bytes 3076
  108.1 9.4 all-to-all-start.1
  117.5 8.8 all-to-all-start.2
  126.2 17.9 all-to-all-start
  129.7 331.3 %all-gather.22.cloned.1.call-start = ((), (), s32[]{:S(2)}) async-start(), calls=%async_computation.23 | async-start | bytes 3932160 | tf_op jit(solution)/shard_map/all_gather | solution.py:206
  171.2 25.4 %copy-start.1 = (bf16[1024,2,64]{0,2,1:T(8,128)(2,1)}, bf16[1024,2,64]{0,2,1:T(8,128)(2,1)S(1)}, u32[]{:S(2)}) copy-start(bf16[1024,2,64]{0,2,1:T(8,128)(2,1)S(1)} %get-tuple-element.626) | copy-start | bytes 786436
  171.3 25.4 %copy-start.3 = (bf16[2,512,2,3,64]{1,4,3,2,0:T(8,128)(2,1)}, bf16[2,512,2,3,64]{1,4,3,2,0:T(8,128)(2,1)S(1)}, u32[]{:S(2)}) copy-start(bf16[2,512,2,3,64]{1,4,3,2,0:T(8,128)(2,1)S(1)} %get-tuple-element.627) | copy-start | bytes 2359300
  171.3 25.4 %copy-start.16 = (bf16[1024,2,64]{0,2,1:T(8,128)(2,1)}, bf16[1024,2,64]{0,2,1:T(8,128)(2,1)S(1)}, u32[]{:S(2)}) copy-start(bf16[1024,2,64]{0,2,1:T(8,128)(2,1)S(1)} %get-tuple-element.635) | copy-start | bytes 786436
  171.3 25.4 %copy-start.39 = (f32[2,2,3,512]{3,2,1,0:T(4,128)}, f32[2,2,3,512]{3,2,1,0:T(4,128)S(1)}, u32[]{:S(2)}) copy-start(f32[2,2,3,512]{3,2,1,0:T(4,128)S(1)} %get-tuple-element.581) | copy-start | bytes 73732
  171.3 25.4 %copy-start.65 = (s32[2]{0:T(128)}, s32[2]{0:T(128)S(1)}, u32[]{:S(2)}) copy-start(s32[2]{0:T(128)S(1)} %get-tuple-element.671) | copy-start | bytes 28
  176.6 15.8 all-to-all-start.3
  180.1 839.9 %all-gather.14.cloned.1.call-start = ((), (), s32[]{:S(2)}) async-start(), calls=%async_computation.15 | async-start | bytes 3932160 | tf_op jit(solution)/shard_map/all_gather | solution.py:172
  198.9 853.6 %all-gather.16.cloned.1.call-start = ((), (), s32[]{:S(2)}) async-start(), calls=%async_computation.16 | async-start | bytes 17694720 | tf_op jit(solution)/shard_map/all_gather | solution.py:189
  199.5 867.1 %all-gather.18.cloned.1.call-start = ((), (), s32[]{:S(2)}) async-start(), calls=%async_computation.17 | async-start | bytes 17694720 | tf_op jit(solution)/shard_map/all_gather | solution.py:190
  200.1 935.9 %all-gather.20.cloned.1.call-start = ((), (), s32[]{:S(2)}) async-start(), calls=%async_computation.19 | async-start | bytes 17694720 | tf_op jit(solution)/shard_map/all_gather | solution.py:212
  200.8 1080.6 %reduce-scatter.10.cloned.1.call-start = ((), (), s32[]{:S(2)}) async-start(), calls=%async_computation.20 | async-start | bytes 7864320 | tf_op jit(solution)/shard_map/reduce_scatter | solution.py:234
  201.4 4.2 collective-permute-start
  211.5 185.1 %collective-permute-start.1 = (bf16[2,192,10,512]{3,1,2,0:T(8,128)(2,1)}, bf16[2,192,10,512]{3,1,2,0:T(8,128)(2,1)}, u32[]{:S(2)}, u32[]{:S(2)}) collective-permute-start(bf16[2,192,10,512]{3,1,2,0:T(8,128)(2,1)} %pad_maximum_fusion.3), channel_id=1, source_target_pairs={{0,2},{1,3},{2,0},{3,1},{4,6},{5,7},{6,4},{7,5},{8,10},{9,11},{10,... | collective-permute-start | bytes 11796488 | tf_op jit(solution)/shard_map/ppermute | solution.py:29
  409.1 597.0 %collective-permute-start.2 = (bf16[4,192,10,512]{3,1,2,0:T(8,128)(2,1)}, bf16[4,192,10,512]{3,1,2,0:T(8,128)(2,1)}, u32[]{:S(2)}, u32[]{:S(2)}) collective-permute-start(bf16[4,192,10,512]{3,1,2,0:T(8,128)(2,1)} %pad_maximum_fusion.2), channel_id=1, source_target_pairs={{0,4},{1,5},{2,6},{3,7},{4,0},{5,1},{6,2},{7,3},{8,12},{9,13},{10,... | collective-permute-start | bytes 23592968 | tf_op jit(solution)/shard_map/ppermute | solution.py:29
  413.1 47.4 %copy-start.62 = (s32[2]{0:T(128)S(1)}, s32[2]{0:T(128)}, u32[]{:S(2)}) copy-start(s32[2]{0:T(128)} %constant.142) | copy-start | bytes 28
  413.1 47.5 %copy-start.61 = (s32[2]{0:T(128)S(1)}, s32[2]{0:T(128)}, u32[]{:S(2)}) copy-start(s32[2]{0:T(128)} %constant.145) | copy-start | bytes 28
  413.1 47.8 %copy-start.31 = (f32[1,1024,8]{1,2,0:T(8,128)S(1)}, f32[1,1024,8]{1,2,0:T(8,128)}, u32[]{:S(2)}) copy-start(f32[1,1024,8]{1,2,0:T(8,128)} %param.22) | copy-start | bytes 98308
  1066.6 16.3 copy-start.5
  1120.1 92.1 %copy-start.41 = (f32[10,205]{1,0:T(8,128)}, f32[10,205]{1,0:T(8,128)S(1)}, u32[]{:S(2)}) copy-start(f32[10,205]{1,0:T(8,128)S(1)} %reshape.325) | copy-start | bytes 24604
  1212.1 116.9 %reduce-scatter.8.cloned.1.call-start = ((), (), s32[]{:S(2)}) async-start(), calls=%async_computation.18 | async-start | bytes 3932160 | tf_op jit(solution)/shard_map/reduce_scatter | solution.py:202
  1264.6 16.8 copy-start.14
  1264.6 16.8 copy-start.44
  1264.6 16.8 copy-start.55
  1269.6 59.5 %copy-start.21 = (bf16[1,256,1536]{2,1,0:T(8,128)(2,1)S(1)}, bf16[1,256,1536]{2,1,0:T(8,128)(2,1)}, u32[]{:S(2)}) copy-start(bf16[1,256,1536]{2,1,0:T(8,128)(2,1)} %param.25) | copy-start | bytes 2359300
  1336.9 19.0 copy-start.2
  1336.9 19.0 copy-start.4
  1337.0 19.0 copy-start.40
  1337.0 19.0 copy-start.66
  1338.1 14.8 all-to-all-start.4
  1413.4 15.0 all-to-all-start.6
  1428.3 14.0 all-to-all-start.5
  1442.3 8.8 all-to-all-start.7
  1445.7 300.2 %reduce-scatter.12.cloned.1.call-start = ((), (), s32[]{:S(2)}) async-start(), calls=%async_computation.21 | async-start | bytes 26763264 | tf_op jit(solution)/shard_map/reduce_scatter | solution.py:322
  1493.7 707.8 %reduce-scatter.16.cloned.1.call-start = ((), (), s32[]{:S(2)}) async-start(), calls=%async_computation.24 | async-start | bytes 53084160
  1628.7 608.4 %reduce-scatter.14.cloned.1.call-start = ((), (), s32[]{:S(2)}) async-start(), calls=%async_computation.22 | async-start | bytes 40960 | tf_op jit(solution)/shard_map/reduce_scatter | solution.py:235
  (53 other events, 280.4 us)
Sparse Core Ops, SparseCore 0:
  11.0 78.1 all-gather.9
  92.3 64.6 all-gather.11
  158.9 46.3 all-gather.21
  207.5 43.6 all-gather.13
  252.7 185.0 all-gather.15
  439.3 346.8 all-gather.17
  787.8 203.8 all-gather.19
  1212.3 69.1 reduce-scatter.9
  1285.0 43.9 reduce-scatter.7
  1493.8 252.0 reduce-scatter.11
  1748.3 453.1 reduce-scatter.15
  2204.7 21.8 reduce-scatter.13
